TPU v7x, 32 devices: a whole 2x2x4 slice. The times are simulated.
32 devices in a mesh: fsdp: 2 (over y), ctx: 16 (over z, x, core).
Axes of the slice: x: 2, y: 2, z: 4, core: 2. Of those that a mesh axis runs over, the one named last changes fastest.
Arguments:
- layer_input: bfloat16 [8, 1024, 1024], P('fsdp', 'ctx'), may hold values from -6 to 6
- output_grad: bfloat16 [8, 1024, 1024], P('fsdp', 'ctx'), may hold values from -6 to 6
- segments: int32 [8, 1024], P('fsdp'), may hold values from 0 to 3, never falling along the last dimension, each value on 1 to 512 neighbouring positions
- assignment: int32 [16], replicated, may hold values from 0 to 15, each once
- first_gain: bfloat16 [1024], P('fsdp'), may hold values from 0.5 to 1.5
- first_bias: bfloat16 [1024], P('fsdp'), may hold values from -1.5 to 1.5
- input_weight: bfloat16 [1024, 3072], P('fsdp'), may hold values from -0.25 to 0.25
- query_bias: bfloat16 [1024], P('fsdp'), may hold values from -2.5 to 2.5
- value_bias: bfloat16 [1024], P('fsdp'), may hold values from -2.5 to 2.5
- output_weight: bfloat16 [1024, 1024], P(None, 'fsdp'), may hold values from -1.5 to 1.5
- output_bias: bfloat16 [1024], P('fsdp'), may hold values from -1.5 to 1.5
- second_gain: bfloat16 [1024], P('fsdp'), may hold values from 0.5 to 1.5
- second_bias: bfloat16 [1024], P('fsdp'), may hold values from -1.5 to 1.5
- expand_weight: bfloat16 [1024, 4096], P('fsdp'), may hold values from -0.1875 to 0.1875
- expand_bias: bfloat16 [4096], P('fsdp'), may hold values from -2.5 to 2.5
- shrink_weight: bfloat16 [4096, 1024], P(None, 'fsdp'), may hold values from -0.09375 to 0.09375
- shrink_bias: bfloat16 [1024], P('fsdp'), may hold values from -1.5 to 1.5
Outputs:
- layer_output: bfloat16 [8, 1024, 1024], P('fsdp', 'ctx')
- input_grad: float32 [8, 1024, 1024], P('fsdp', 'ctx')
- first_gain_grad: float32 [1024], P('fsdp')
- first_bias_grad: float32 [1024], P('fsdp')
- input_weight_grad: float32 [1024, 3072], P('fsdp')
- query_bias_grad: float32 [1024], P('fsdp')
- value_bias_grad: float32 [1024], P('fsdp')
- output_weight_grad: float32 [1024, 1024], P(None, 'fsdp')
- output_bias_grad: float32 [1024], P('fsdp')
- second_gain_grad: float32 [1024], P('fsdp')
- second_bias_grad: float32 [1024], P('fsdp')
- expand_weight_grad: float32 [1024, 4096], P('fsdp')
- expand_bias_grad: float32 [4096], P('fsdp')
- shrink_weight_grad: float32 [4096, 1024], P(None, 'fsdp')
- shrink_bias_grad: float32 [1024], P('fsdp')
Inputs may be any that keep to these rules, and one draw needn't show every extreme that they name: `segments`: in each sequence, in the order of positions, the document numbers never fall; each document has 1 to 512 positions and one has exactly 512. A permutation: index i of ctx holds the blocks assignment[i] and 31 - assignment[i] of every sequence.
All inputs are finite; a program needn't handle non-finite values.
Results may differ from a plain program's by a relative error of at most 0.012.
The roundings to bfloat16 on the way count: a program that leaves them out, or rounds other values in their place, can miss the bound.
Values may be sent and summed in bfloat16 or wider, within the bound.
No kernel may reach another device: no remote copies, remote signals or barrier semaphores. Data moves between devices by JAX's collectives and lax.ppermute only.
A program may use at most 320 MiB of HBM per device.

v0:
```python
import math
import jax
import jax.numpy as jnp
from jax import lax
from jax.sharding import PartitionSpec as P

HEADS = 16
MICRO = 2
EPSILON = 1e-05
MASKED = -1000000000.0


def layer_norm(inputs, norm_gain, norm_bias):
    center = inputs - jnp.mean(inputs, axis=-1, keepdims=True)
    spread = jnp.mean(center * center, axis=-1, keepdims=True)
    return center * lax.rsqrt(spread + EPSILON) * norm_gain + norm_bias


def gelu_tanh(inputs):
    return jax.nn.gelu(inputs, approximate=True)


def key_places(assignment, row_count, length):
    pairs = assignment.shape[0]
    span_len = row_count // 2
    places = jnp.arange(length, dtype=jnp.int32)
    owner = places // row_count
    within = places % row_count
    match = owner[:, None] == jnp.arange(pairs, dtype=jnp.int32)[None, :]
    paired = jnp.sum(jnp.where(match, assignment[None, :], 0), axis=1)
    early = paired * span_len + within
    later = (2 * pairs - 1 - paired) * span_len + within - span_len
    return jnp.where(within < span_len, early, later)


def masked_scores(queries, key_rows, query_place, key_place, query_doc, key_doc, inv_root):
    scores = (
        jnp.einsum("sqhd,skhd->shqk", queries, key_rows, preferred_element_type=jnp.float32)
        * inv_root
    )
    allowed = (key_place[None, None, :] <= query_place[None, :, None]) & (
        key_doc[:, None, :] == query_doc[:, :, None]
    )
    return jnp.where(allowed[:, None], scores, MASKED)


def one_batch(weights, layer_input, output_grad, segments, places, own_places):
    (
        first_gain,
        first_bias,
        input_weight,
        query_bias,
        value_bias,
        output_weight,
        output_bias,
        second_gain,
        second_bias,
        expand_weight,
        expand_bias,
        shrink_weight,
        shrink_bias,
    ) = weights
    seq_count, row_count, features = layer_input.shape
    head_count = HEADS
    head_size = features // head_count
    inv_root = 1.0 / math.sqrt(head_size)
    length = places.shape[0]
    size_k = min(512, length)
    blocks = length // size_k
    key_docs = jnp.take(segments, places, axis=1)
    own_docs = jnp.take(segments, own_places, axis=1)
    inputs = layer_input.astype(jnp.float32)
    normed, first_pull = jax.vjp(
        layer_norm, inputs, first_gain.astype(jnp.float32), first_bias.astype(jnp.float32)
    )
    normed = normed.astype(jnp.bfloat16)
    joined = jnp.einsum("srd,de->sre", normed, input_weight, preferred_element_type=jnp.float32)
    queries = (joined[..., :features] + query_bias.astype(jnp.float32)).astype(jnp.bfloat16)
    key_value = jnp.concatenate(
        [
            joined[..., features : 2 * features],
            joined[..., 2 * features :] + value_bias.astype(jnp.float32),
        ],
        axis=-1,
    ).astype(jnp.bfloat16)
    gathered = lax.all_gather(key_value, "ctx", axis=1, tiled=True)
    query_heads = queries.reshape(seq_count, row_count, head_count, head_size)

    def key_block(number):
        offset = number * size_k
        pieces = lax.dynamic_slice_in_dim(gathered, offset, size_k, 1)
        key_rows = pieces[..., :features].reshape(seq_count, size_k, head_count, head_size)
        value_rows = pieces[..., features:].reshape(seq_count, size_k, head_count, head_size)
        block_places = lax.dynamic_slice_in_dim(places, offset, size_k, 0)
        block_docs = lax.dynamic_slice_in_dim(key_docs, offset, size_k, 1)
        scores = masked_scores(
            query_heads, key_rows, own_places, block_places, own_docs, block_docs, inv_root
        )
        return (key_rows, value_rows, scores)

    def max_sum(number, running):
        scores = key_block(number)[2]
        highest = jnp.maximum(running[0], jnp.max(scores, axis=-1))
        totals = running[1] * jnp.exp(running[0] - highest) + jnp.sum(
            jnp.exp(scores - highest[..., None]), axis=-1
        )
        return (highest, totals)

    stats_shape = (seq_count, head_count, row_count)
    highest, totals = lax.fori_loop(
        0,
        blocks,
        max_sum,
        (jnp.full(stats_shape, MASKED, jnp.float32), jnp.zeros(stats_shape, jnp.float32)),
    )
    log_total = highest + jnp.log(totals)

    def mix_values(number, running):
        pieces = key_block(number)
        probs_low = jnp.exp(pieces[2] - log_total[..., None]).astype(jnp.bfloat16)
        return running + jnp.einsum(
            "shqk,skhd->sqhd", probs_low, pieces[1], preferred_element_type=jnp.float32
        )

    mixed_heads = lax.fori_loop(
        0, blocks, mix_values, jnp.zeros((seq_count, row_count, head_count, head_size), jnp.float32)
    )
    mixed_low = mixed_heads.reshape(seq_count, row_count, features).astype(jnp.bfloat16)
    residual = (
        inputs
        + jnp.einsum("sre,ed->srd", mixed_low, output_weight, preferred_element_type=jnp.float32)
        + output_bias.astype(jnp.float32)
    )
    normed_two, second_pull = jax.vjp(
        layer_norm, residual, second_gain.astype(jnp.float32), second_bias.astype(jnp.float32)
    )
    normed_two = normed_two.astype(jnp.bfloat16)
    hidden = jnp.einsum(
        "srd,df->srf", normed_two, expand_weight, preferred_element_type=jnp.float32
    ) + expand_bias.astype(jnp.float32)
    active, gelu_pull = jax.vjp(gelu_tanh, hidden)
    active = active.astype(jnp.bfloat16)
    layer_output = (
        residual
        + jnp.einsum("srf,fd->srd", active, shrink_weight, preferred_element_type=jnp.float32)
        + shrink_bias.astype(jnp.float32)
    ).astype(jnp.bfloat16)
    cotangent = output_grad.astype(jnp.float32)
    shrink_weight_grad = jnp.einsum(
        "srf,srd->fd", active, output_grad, preferred_element_type=jnp.float32
    )
    shrink_bias_grad = jnp.sum(cotangent, axis=(0, 1))
    hidden_grad = gelu_pull(
        jnp.einsum("srd,fd->srf", output_grad, shrink_weight, preferred_element_type=jnp.float32)
    )[0].astype(jnp.bfloat16)
    expand_weight_grad = jnp.einsum(
        "srd,srf->df", normed_two, hidden_grad, preferred_element_type=jnp.float32
    )
    expand_bias_grad = jnp.sum(hidden_grad.astype(jnp.float32), axis=(0, 1))
    second_grads = second_pull(
        jnp.einsum("srf,df->srd", hidden_grad, expand_weight, preferred_element_type=jnp.float32)
    )
    residual_grad = cotangent + second_grads[0]
    branch_grad = residual_grad.astype(jnp.bfloat16)
    output_weight_grad = jnp.einsum(
        "sre,srd->ed", mixed_low, branch_grad, preferred_element_type=jnp.float32
    )
    output_bias_grad = jnp.sum(branch_grad.astype(jnp.float32), axis=(0, 1))
    mixed_flat = jnp.einsum(
        "srd,ed->sre", branch_grad, output_weight, preferred_element_type=jnp.float32
    ).astype(jnp.bfloat16)
    mixed_grad = mixed_flat.reshape(seq_count, row_count, head_count, head_size)

    def prob_grads(pieces):
        probs = jnp.exp(pieces[2] - log_total[..., None])
        prob_grad = jnp.einsum(
            "sqhd,skhd->shqk", mixed_grad, pieces[1], preferred_element_type=jnp.float32
        )
        return (probs, prob_grad)

    def delta_sum(number, running):
        probs, prob_grad = prob_grads(key_block(number))
        return running + jnp.sum(probs * prob_grad, axis=-1)

    deltas = lax.fori_loop(0, blocks, delta_sum, jnp.zeros(stats_shape, jnp.float32))
    query_zero = jnp.zeros((seq_count, row_count, head_count, head_size), jnp.float32)

    def key_grads(number, running):
        pieces = key_block(number)
        probs, prob_grad = prob_grads(pieces)
        score_grad = (probs * (prob_grad - deltas[..., None])).astype(jnp.bfloat16)
        query_grad = (
            running[0]
            + jnp.einsum(
                "shqk,skhd->sqhd", score_grad, pieces[0], preferred_element_type=jnp.float32
            )
            * inv_root
        )
        key_grad = (
            jnp.einsum(
                "shqk,sqhd->skhd", score_grad, query_heads, preferred_element_type=jnp.float32
            )
            * inv_root
        )
        value_grad = jnp.einsum(
            "shqk,sqhd->skhd",
            probs.astype(jnp.bfloat16),
            mixed_grad,
            preferred_element_type=jnp.float32,
        )
        joined_grad = jnp.concatenate(
            [
                key_grad.reshape(seq_count, size_k, features),
                value_grad.reshape(seq_count, size_k, features),
            ],
            axis=-1,
        )
        buffer = lax.dynamic_update_slice_in_dim(running[1], joined_grad, number * size_k, 1)
        return (query_grad, buffer)

    query_grad, buffer = lax.fori_loop(
        0,
        blocks,
        key_grads,
        (query_zero, jnp.zeros((seq_count, length, 2 * features), jnp.float32)),
    )
    key_value_grad = lax.psum_scatter(buffer, "ctx", scatter_dimension=1, tiled=True).astype(
        jnp.bfloat16
    )
    query_low = query_grad.reshape(seq_count, row_count, features).astype(jnp.bfloat16)
    joined_low = jnp.concatenate([query_low, key_value_grad], axis=-1)
    input_weight_grad = jnp.einsum(
        "srd,sre->de", normed, joined_low, preferred_element_type=jnp.float32
    )
    query_bias_grad = jnp.sum(query_low.astype(jnp.float32), axis=(0, 1))
    value_bias_grad = jnp.sum(key_value_grad[..., features:].astype(jnp.float32), axis=(0, 1))
    first_grads = first_pull(
        jnp.einsum("sre,de->srd", joined_low, input_weight, preferred_element_type=jnp.float32)
    )
    input_grad = residual_grad + first_grads[0]
    grads = (
        first_grads[1],
        first_grads[2],
        input_weight_grad,
        query_bias_grad,
        value_bias_grad,
        output_weight_grad,
        output_bias_grad,
        second_grads[1],
        second_grads[2],
        expand_weight_grad,
        expand_bias_grad,
        shrink_weight_grad,
        shrink_bias_grad,
    )
    return (layer_output, input_grad, grads)


def body(
    layer_input,
    output_grad,
    segments,
    assignment,
    first_gain,
    first_bias,
    input_weight,
    query_bias,
    value_bias,
    output_weight,
    output_bias,
    second_gain,
    second_bias,
    expand_weight,
    expand_bias,
    shrink_weight,
    shrink_bias,
):
    row_count = layer_input.shape[1]
    length = row_count * lax.axis_size("ctx")
    places = key_places(assignment, row_count, length)
    own_places = lax.dynamic_slice_in_dim(places, lax.axis_index("ctx") * row_count, row_count, 0)
    batch_seqs = layer_input.shape[0] // MICRO
    outputs = []
    input_grads = []
    summed = None
    for micro_turn in range(MICRO):
        weights = (
            lax.all_gather(first_gain, "fsdp", axis=0, tiled=True),
            lax.all_gather(first_bias, "fsdp", axis=0, tiled=True),
            lax.all_gather(input_weight, "fsdp", axis=0, tiled=True),
            lax.all_gather(query_bias, "fsdp", axis=0, tiled=True),
            lax.all_gather(value_bias, "fsdp", axis=0, tiled=True),
            lax.all_gather(output_weight, "fsdp", axis=1, tiled=True),
            lax.all_gather(output_bias, "fsdp", axis=0, tiled=True),
            lax.all_gather(second_gain, "fsdp", axis=0, tiled=True),
            lax.all_gather(second_bias, "fsdp", axis=0, tiled=True),
            lax.all_gather(expand_weight, "fsdp", axis=0, tiled=True),
            lax.all_gather(expand_bias, "fsdp", axis=0, tiled=True),
            lax.all_gather(shrink_weight, "fsdp", axis=1, tiled=True),
            lax.all_gather(shrink_bias, "fsdp", axis=0, tiled=True),
        )
        lower = micro_turn * batch_seqs
        upper = lower + batch_seqs
        result = one_batch(
            weights,
            layer_input[lower:upper],
            output_grad[lower:upper],
            segments[lower:upper],
            places,
            own_places,
        )
        outputs.append(result[0])
        input_grads.append(result[1])
        batch_grads = result[2]
        summed = (
            batch_grads
            if summed is None
            else tuple((first + second for first, second in zip(summed, batch_grads)))
        )
    summed = lax.psum(
        (
            lax.psum_scatter(summed[0], "fsdp", scatter_dimension=0, tiled=True),
            lax.psum_scatter(summed[1], "fsdp", scatter_dimension=0, tiled=True),
            lax.psum_scatter(summed[2], "fsdp", scatter_dimension=0, tiled=True),
            lax.psum_scatter(summed[3], "fsdp", scatter_dimension=0, tiled=True),
            lax.psum_scatter(summed[4], "fsdp", scatter_dimension=0, tiled=True),
            lax.psum_scatter(summed[5], "fsdp", scatter_dimension=1, tiled=True),
            lax.psum_scatter(summed[6], "fsdp", scatter_dimension=0, tiled=True),
            lax.psum_scatter(summed[7], "fsdp", scatter_dimension=0, tiled=True),
            lax.psum_scatter(summed[8], "fsdp", scatter_dimension=0, tiled=True),
            lax.psum_scatter(summed[9], "fsdp", scatter_dimension=0, tiled=True),
            lax.psum_scatter(summed[10], "fsdp", scatter_dimension=0, tiled=True),
            lax.psum_scatter(summed[11], "fsdp", scatter_dimension=1, tiled=True),
            lax.psum_scatter(summed[12], "fsdp", scatter_dimension=0, tiled=True),
        ),
        "ctx",
    )
    return (
        jnp.concatenate(outputs, axis=0),
        jnp.concatenate(input_grads, axis=0),
        summed[0],
        summed[1],
        summed[2],
        summed[3],
        summed[4],
        summed[5],
        summed[6],
        summed[7],
        summed[8],
        summed[9],
        summed[10],
        summed[11],
        summed[12],
    )


def solution(mesh):
    return jax.shard_map(
        body,
        mesh=mesh,
        in_specs=(
            P("fsdp", "ctx", None),
            P("fsdp", "ctx", None),
            P("fsdp", None),
            P(),
            P("fsdp"),
            P("fsdp"),
            P("fsdp", None),
            P("fsdp"),
            P("fsdp"),
            P(None, "fsdp"),
            P("fsdp"),
            P("fsdp"),
            P("fsdp"),
            P("fsdp", None),
            P("fsdp"),
            P(None, "fsdp"),
            P("fsdp"),
        ),
        out_specs=(
            P("fsdp", "ctx", None),
            P("fsdp", "ctx", None),
            P("fsdp"),
            P("fsdp"),
            P("fsdp", None),
            P("fsdp"),
            P("fsdp"),
            P(None, "fsdp"),
            P("fsdp"),
            P("fsdp"),
            P("fsdp"),
            P("fsdp", None),
            P("fsdp"),
            P(None, "fsdp"),
            P("fsdp"),
        ),
        check_vma=False,
    )
```

profile of v0, /device:TPU:0, one launch (start us, length us, event | category | flops | bytes accessed | tf_op | source)
XLA Modules:
  0.0 2027.5 jit_solution(2020608010366841230)
XLA Ops:
  8.0 5.3 all-gather.1
  27.5 65.3 %all-gather.15.cloned.1.call-done = bf16[1024,3072]{1,0:T(8,128)(2,1)} async-done(((bf16[512,3072]{1,0:T(8,128)(2,1)}), bf16[1024,3072]{1,0:T(8,128)(2,1)}) %all-gather.15.cloned.1.call-update) | async-done | bytes 6291472 | tf_op jit(solution)/shard_map/all_gather | solution.py:290
  123.6 4.8 all-gather.5
  131.0 43.7 %all-gather.25.cloned.1.call-done = bf16[2,1024,2048]{2,1,0:T(8,128)(2,1)} async-done(((bf16[2,64,2048]{2,1,0:T(8,128)(2,1)}), bf16[2,1024,2048]{2,1,0:T(8,128)(2,1)}) %all-gather.25.cloned.1.call-update) | async-done | bytes 8388624 | tf_op jit(solution)/shard_map/all_gather | solution.py:86
  174.7 12.0 copy.147
  186.6 16.3 while.122
  203.0 17.4 while.123
  215.8 4.5 fusion.337
  222.4 28.2 %all-gather.17.cloned.1.call-done = bf16[2,1024,2048]{2,1,0:T(8,128)(2,1)} async-done(((bf16[2,64,2048]{2,1,0:T(8,128)(2,1)}), bf16[2,1024,2048]{2,1,0:T(8,128)(2,1)}) %all-gather.17.cloned.1.call-update) | async-done | bytes 8388624 | tf_op jit(solution)/shard_map/all_gather | solution.py:86
  250.6 12.0 copy.137
  262.6 16.3 while.120
  278.9 18.0 while.121
  291.7 5.0 fusion.329
  303.5 85.4 %all-gather.21.cloned.1.call-done = bf16[1024,4096]{1,0:T(8,128)(2,1)} async-done(((bf16[512,4096]{1,0:T(8,128)(2,1)}), bf16[1024,4096]{1,0:T(8,128)(2,1)}) %all-gather.21.cloned.1.call-update) | async-done | bytes 8388624 | tf_op jit(solution)/shard_map/all_gather | solution.py:297
  388.9 6.3 fusion.81
  397.9 96.4 %all-gather.23.cloned.1.call-done = bf16[4096,1024]{1,0:T(8,128)(2,1)} async-done(((bf16[4096,512]{1,0:T(8,128)(2,1)}), bf16[4096,1024]{1,0:T(8,128)(2,1)}) %all-gather.23.cloned.1.call-update) | async-done | bytes 8388624 | tf_op jit(solution)/shard_map/all_gather | solution.py:299
  494.3 8.5 convert_reduce_fusion
  503.7 6.4 fusion.62
  510.2 4.4 convert_reduce_fusion.1
  523.0 10.5 while.126
  533.5 7.9 broadcast.727.clone2
  541.4 66.1 %while.127 = (s32[]{:T(128)}, f32[2,64,16,64]{1,3,2,0:T(8,128)}, f32[2,1024,2048]{2,1,0:T(8,128)}, bf16[2,1024,2048]{1,2,0:T(8,128)(2,1)}, s32[1024]{0:T(1024)S(...) while((s32[]{:T(128)}, f32[2,64,16,64]{1,3,2,0:T(8,128)}, ...), condition=%wide.region_37.40_spmd.clone, body=%wide.region_36.39_spmd.clone.sunk | while | flops 685277184 | bytes 136621136 | solution.py:221
  557.9 8.8 copy.231
  566.7 7.8 constant_dynamic-update-slice_fusion.5
  591.0 8.8 copy.231
  599.8 7.7 constant_dynamic-update-slice_fusion.5
  612.6 11.8 while.124
  624.5 10.5 broadcast.727.clone2.1
  635.0 66.7 %while.125 = (s32[]{:T(128)}, f32[2,64,16,64]{1,3,2,0:T(8,128)}, f32[2,1024,2048]{2,1,0:T(8,128)}, bf16[2,1024,2048]{1,2,0:T(8,128)(2,1)}, s32[1024]{0:T(1024)S(...) while((s32[]{:T(128)}, f32[2,64,16,64]{1,3,2,0:T(8,128)}, ...), condition=%wide.region_27.30_spmd.clone, body=%wide.region_26.29_spmd.clone.sunk | while | flops 685277184 | bytes 136621136 | solution.py:221
  651.6 8.9 copy.230
  660.5 7.8 constant_dynamic-update-slice_fusion.4
  685.1 8.8 copy.230
  693.9 7.8 constant_dynamic-update-slice_fusion.4
  710.3 8.3 bitcast_add_fusion.1
  723.6 9.8 bitcast_add_fusion
  737.3 48.9 %reduce-scatter.9.cloned.1.call-done = f32[2,64,2048]{2,1,0:T(8,128)} async-done(((f32[2,1024,2048]{2,1,0:T(8,128)}), f32[2,64,2048]{2,1,0:T(8,128)}) %reduce-scatter.9.cloned.1.call-update) | async-done | bytes 1048592 | tf_op jit(solution)/shard_map/reduce_scatter | solution.py:227
  787.5 180.4 %reduce-scatter.7.cloned.1.call-done = f32[2,64,2048]{2,1,0:T(8,128)} async-done(((f32[2,1024,2048]{2,1,0:T(8,128)}), f32[2,64,2048]{2,1,0:T(8,128)}) %reduce-scatter.7.cloned.1.call-update) | async-done | bytes 1048592 | tf_op jit(solution)/shard_map/reduce_scatter | solution.py:227
  971.3 6.8 bitcast_add_fusion.2
  978.1 46.0 %reduce-scatter.13.cloned.1.call-done = f32[1024,512]{1,0:T(8,128)} async-done(((f32[1024,1024]{1,0:T(8,128)}), f32[1024,512]{1,0:T(8,128)}) %reduce-scatter.13.cloned.1.call-update) | async-done | bytes 2097168 | tf_op jit(solution)/shard_map/reduce_scatter | solution.py:327
  1024.2 191.4 %reduce-scatter.15.cloned.1.call-done = f32[512,4096]{1,0:T(8,128)} async-done(((f32[1024,4096]{1,0:T(8,128)}), f32[512,4096]{1,0:T(8,128)}) %reduce-scatter.15.cloned.1.call-update) | async-done | bytes 8388624 | tf_op jit(solution)/shard_map/reduce_scatter | solution.py:331
  1215.6 191.5 %reduce-scatter.17.cloned.1.call-done = f32[4096,512]{1,0:T(8,128)} async-done(((f32[4096,1024]{1,0:T(8,128)}), f32[4096,512]{1,0:T(8,128)}) %reduce-scatter.17.cloned.1.call-update) | async-done | bytes 8388624 | tf_op jit(solution)/shard_map/reduce_scatter | solution.py:333
  1407.0 146.8 %reduce-scatter.11.cloned.1.call-done = f32[512,3072]{1,0:T(8,128)} async-done(((f32[1024,3072]{1,0:T(8,128)}), f32[512,3072]{1,0:T(8,128)}) %reduce-scatter.11.cloned.1.call-update) | async-done | bytes 6291472 | tf_op jit(solution)/shard_map/reduce_scatter | solution.py:324
  1561.0 5.9 fusion.134
  1566.9 5.1 fusion.137
  1579.2 7.4 all-reduce.11
  1587.2 63.6 %all-reduce.9 = (f32[512]{0:T(512)}, f32[512]{0:T(512)}, f32[512]{0:T(512)}, f32[512]{0:T(512)}, f32[512]{0:T(512)}, /*index=5*/f32[512]{0:T(512)}, f32[512]{0:T(512)}, f32[2048]{0:T(1024)}, f32[512]{0:T(512)}) all-reduce(f32[512]{0:T(512)S(1)} %dynamic-slice.1, ...), channel_id=1, replica_groups=mesh['fsdp'=2,'ctx'=16] {'ctx'}, use_global_device_ids=true, to_apply=%region_44.47 | all-reduce | flops 6144 | bytes 49152 | tf_op jit(solution)/shard_map/psum | solution.py:320
  1652.4 350.5 %all-reduce.14.cloned.1.call-done = (f32[512,3072]{1,0:T(8,128)}, f32[1024,512]{1,0:T(8,128)}, f32[512,4096]{1,0:T(8,128)}, f32[4096,512]{1,0:T(8,128)}) async-done(((f32[512,3072]{1,0:T(8,128)}, f32[1024,512]{1,0:T(8,128)}, f32[512,4096]{1,0:T(8,128)}, f32[4096,512]{1,0:T(8,128)}), (f32[512,3072]{1,0:T(8,128)}, f32[1024,512]{1,0:T(8,128)}, f32[512,4096]{1,0:T(8,128)}, ...) | async-done | bytes 25165840 | tf_op jit(solution)/shard_map/psum | solution.py:320
  2003.0 6.9 copy.298
  (558 shorter events, 266.3 us)
Async XLA Ops:
  7.2 14.8 copy-start.102
  7.2 19.2 copy-start.14
  7.2 85.5 %all-gather.15.cloned.1.call-start = ((), (), s32[]{:S(2)}) async-start(), calls=%async_computation.6 | async-start | bytes 9437184 | tf_op jit(solution)/shard_map/all_gather | solution.py:290
  8.0 166.7 %all-gather.25.cloned.1.call-start = ((), (), s32[]{:S(2)}) async-start(), calls=%async_computation.11 | async-start | bytes 8912896 | tf_op jit(solution)/shard_map/all_gather | solution.py:86
  13.3 83.5 %copy-start.53 = (f32[2,1,512]{2,1,0:T(1,128)}, f32[2,1,512]{2,1,0:T(1,128)S(1)}, u32[]{:S(2)}) copy-start(f32[2,1,512]{2,1,0:T(1,128)S(1)} %convert_element_type.246) | copy-start | bytes 12292
  17.7 79.2 %copy-start.48 = (f32[2,1,512]{2,1,0:T(1,128)}, f32[2,1,512]{2,1,0:T(1,128)S(1)}, u32[]{:S(2)}) copy-start(f32[2,1,512]{2,1,0:T(1,128)S(1)} %convert_element_type.245) | copy-start | bytes 12292
  26.6 70.2 %copy-start.67 = (f32[2,64]{1,0:T(2,128)}, f32[2,64]{1,0:T(2,128)S(1)}, u32[]{:S(2)}) copy-start(f32[2,64]{1,0:T(2,128)S(1)} %get-tuple-element.2158) | copy-start | bytes 1540
  26.6 70.3 %copy-start.69 = (f32[2,64]{1,0:T(2,128)}, f32[2,64]{1,0:T(2,128)S(1)}, u32[]{:S(2)}) copy-start(f32[2,64]{1,0:T(2,128)S(1)} %get-tuple-element.2159) | copy-start | bytes 1540
  26.9 69.9 %copy-start.96 = (f32[2,64]{1,0:T(2,128)}, f32[2,64]{1,0:T(2,128)S(1)}, u32[]{:S(2)}) copy-start(f32[2,64]{1,0:T(2,128)S(1)} %get-tuple-element.1907) | copy-start | bytes 1540
  27.5 69.3 %copy-start.73 = (f32[2,64]{1,0:T(2,128)}, f32[2,64]{1,0:T(2,128)S(1)}, u32[]{:S(2)}) copy-start(f32[2,64]{1,0:T(2,128)S(1)} %fusion.198) | copy-start | bytes 1540
  27.5 69.4 %copy-start.75 = (f32[2,64]{1,0:T(2,128)}, f32[2,64]{1,0:T(2,128)S(1)}, u32[]{:S(2)}) copy-start(f32[2,64]{1,0:T(2,128)S(1)} %fusion.196) | copy-start | bytes 1540
  99.6 151.1 %all-gather.17.cloned.1.call-start = ((), (), s32[]{:S(2)}) async-start(), calls=%async_computation.7 | async-start | bytes 8912896 | tf_op jit(solution)/shard_map/all_gather | solution.py:86
  100.5 198.8 %all-gather.19.cloned.1.call-start = ((), (), s32[]{:S(2)}) async-start(), calls=%async_computation.8 | async-start | bytes 3145728 | tf_op jit(solution)/shard_map/all_gather | solution.py:293
  101.1 287.8 %all-gather.21.cloned.1.call-start = ((), (), s32[]{:S(2)}) async-start(), calls=%async_computation.9 | async-start | bytes 12582912 | tf_op jit(solution)/shard_map/all_gather | solution.py:297
  101.7 392.6 %all-gather.23.cloned.1.call-start = ((), (), s32[]{:S(2)}) async-start(), calls=%async_computation.10 | async-start | bytes 12582912 | tf_op jit(solution)/shard_map/all_gather | solution.py:299
  102.3 12.6 copy-start.98
  102.3 683.9 %reduce-scatter.9.cloned.1.call-start = ((), (), s32[]{:S(2)}) async-start(), calls=%async_computation.13 | async-start | bytes 17825792 | tf_op jit(solution)/shard_map/reduce_scatter | solution.py:227
  102.5 16.8 copy-start.104
  102.5 21.1 %copy-start.105 = (bf16[512]{0:T(512)(128)(2,1)S(1)}, bf16[512]{0:T(512)(128)(2,1)}, u32[]{:S(2)}) copy-start(bf16[512]{0:T(512)(128)(2,1)} %param.48) | copy-start | bytes 3076
  123.6 271.6 %copy-start.55 = (f32[2,1,512]{2,1,0:T(1,128)}, f32[2,1,512]{2,1,0:T(1,128)S(1)}, u32[]{:S(2)}) copy-start(f32[2,1,512]{2,1,0:T(1,128)S(1)} %convert_element_type.251) | copy-start | bytes 12292
  128.5 389.8 %copy-start.50 = (f32[2,1,512]{2,1,0:T(1,128)}, f32[2,1,512]{2,1,0:T(1,128)S(1)}, u32[]{:S(2)}) copy-start(f32[2,1,512]{2,1,0:T(1,128)S(1)} %convert_element_type.250) | copy-start | bytes 12292
  130.8 55.8 %copy-start.39 = (bf16[2,64,16,64]{3,2,1,0:T(8,128)(2,1)}, bf16[2,64,16,64]{3,2,1,0:T(8,128)(2,1)S(1)}, u32[]{:S(2)}) copy-start(bf16[2,64,16,64]{3,2,1,0:T(8,128)(2,1)S(1)} %reshape.630) | copy-start | bytes 786436
  302.1 216.1 %copy-start.63 = (f32[2,64]{1,0:T(2,128)}, f32[2,64]{1,0:T(2,128)S(1)}, u32[]{:S(2)}) copy-start(f32[2,64]{1,0:T(2,128)S(1)} %broadcast_multiply_fusion) | copy-start | bytes 1540
  303.2 215.1 %copy-start.20 = (f32[2,64,1024]{2,1,0:T(8,128)}, f32[2,64,1024]{2,1,0:T(8,128)S(1)}, u32[]{:S(2)}) copy-start(f32[2,64,1024]{2,1,0:T(8,128)S(1)} %get-tuple-element.2151) | copy-start | bytes 1572868
  303.2 215.1 %copy-start.65 = (f32[2,64]{1,0:T(2,128)}, f32[2,64]{1,0:T(2,128)S(1)}, u32[]{:S(2)}) copy-start(f32[2,64]{1,0:T(2,128)S(1)} %broadcast_multiply_fusion.2) | copy-start | bytes 1540
  303.4 214.9 %copy-start.71 = (f32[2,64]{1,0:T(2,128)}, f32[2,64]{1,0:T(2,128)S(1)}, u32[]{:S(2)}) copy-start(f32[2,64]{1,0:T(2,128)S(1)} %fusion.199) | copy-start | bytes 1540
  303.5 214.9 %copy-start.77 = (f32[2,64]{1,0:T(2,128)}, f32[2,64]{1,0:T(2,128)S(1)}, u32[]{:S(2)}) copy-start(f32[2,64]{1,0:T(2,128)S(1)} %fusion.197) | copy-start | bytes 1540
  494.3 15.9 copy-start.108
  503.7 10.9 slice-start
  607.5 360.4 %reduce-scatter.7.cloned.1.call-start = ((), (), s32[]{:S(2)}) async-start(), calls=%async_computation.12 | async-start | bytes 17825792 | tf_op jit(solution)/shard_map/reduce_scatter | solution.py:227
  701.8 322.4 %reduce-scatter.13.cloned.1.call-start = ((), (), s32[]{:S(2)}) async-start(), calls=%async_computation.15 | async-start | bytes 6291456 | tf_op jit(solution)/shard_map/reduce_scatter | solution.py:327
  706.5 509.1 %reduce-scatter.15.cloned.1.call-start = ((), (), s32[]{:S(2)}) async-start(), calls=%async_computation.16 | async-start | bytes 25165824 | tf_op jit(solution)/shard_map/reduce_scatter | solution.py:331
  718.6 688.4 %reduce-scatter.17.cloned.1.call-start = ((), (), s32[]{:S(2)}) async-start(), calls=%async_computation.17 | async-start | bytes 25165824 | tf_op jit(solution)/shard_map/reduce_scatter | solution.py:333
  733.5 820.3 %reduce-scatter.11.cloned.1.call-start = ((), (), s32[]{:S(2)}) async-start(), calls=%async_computation.14 | async-start | bytes 18874368 | tf_op jit(solution)/shard_map/reduce_scatter | solution.py:324
  737.0 232.2 %copy-start.16 = (bf16[4,64,1024]{2,1,0:T(8,128)(2,1)S(1)}, bf16[4,64,1024]{2,1,0:T(8,128)(2,1)}, u32[]{:S(2)}) copy-start(bf16[4,64,1024]{2,1,0:T(8,128)(2,1)} %param.37) | copy-start | bytes 1572868
  737.0 232.2 %copy-start.49 = (f32[2,1,512]{2,1,0:T(1,128)S(1)}, f32[2,1,512]{2,1,0:T(1,128)}, u32[]{:S(2)}) copy-start(f32[2,1,512]{2,1,0:T(1,128)} %copy-done.48) | copy-start | bytes 12292
  737.1 232.2 %copy-start.54 = (f32[2,1,512]{2,1,0:T(1,128)S(1)}, f32[2,1,512]{2,1,0:T(1,128)}, u32[]{:S(2)}) copy-start(f32[2,1,512]{2,1,0:T(1,128)} %copy-done.53) | copy-start | bytes 12292
  737.1 232.2 %copy-start.70 = (f32[2,64]{1,0:T(2,128)S(1)}, f32[2,64]{1,0:T(2,128)}, u32[]{:S(2)}) copy-start(f32[2,64]{1,0:T(2,128)} %copy-done.69) | copy-start | bytes 1540
  737.1 232.2 %copy-start.76 = (f32[2,64]{1,0:T(2,128)S(1)}, f32[2,64]{1,0:T(2,128)}, u32[]{:S(2)}) copy-start(f32[2,64]{1,0:T(2,128)} %copy-done.75) | copy-start | bytes 1540
  787.5 785.4 %copy-start.41 = (bf16[2,64,2048]{2,1,0:T(8,128)(2,1)}, bf16[2,64,2048]{2,1,0:T(8,128)(2,1)S(1)}, u32[]{:S(2)}) copy-start(bf16[2,64,2048]{2,1,0:T(8,128)(2,1)S(1)} %convert_element_type.236) | copy-start | bytes 1572868
  969.3 605.8 %copy-start.43 = (bf16[2,64,2048]{2,1,0:T(8,128)(2,1)}, bf16[2,64,2048]{2,1,0:T(8,128)(2,1)S(1)}, u32[]{:S(2)}) copy-start(bf16[2,64,2048]{2,1,0:T(8,128)(2,1)S(1)} %convert_element_type.229) | copy-start | bytes 1572868
  978.1 1024.9 %all-reduce.14.cloned.1.call-start = ((), (), s32[]{:S(2)}) async-start(), calls=%async_computation.18 | async-start | bytes 50331648 | tf_op jit(solution)/shard_map/psum | solution.py:320
  1561.0 11.9 slice-start.2
  1577.5 73.4 %copy-start.31 = (bf16[4,64,1024]{2,1,0:T(8,128)(2,1)S(1)}, bf16[4,64,1024]{2,1,0:T(8,128)(2,1)}, u32[]{:S(2)}) copy-start(bf16[4,64,1024]{2,1,0:T(8,128)(2,1)} %param.38) | copy-start | bytes 1572868
  1577.5 73.4 %copy-start.36 = (f32[2,64,1024]{2,1,0:T(8,128)S(1)}, f32[2,64,1024]{2,1,0:T(8,128)}, u32[]{:S(2)}) copy-start(f32[2,64,1024]{2,1,0:T(8,128)} %copy-done.35) | copy-start | bytes 1572868
  1577.5 73.4 %copy-start.38 = (f32[2,64,1024]{2,1,0:T(8,128)S(1)}, f32[2,64,1024]{2,1,0:T(8,128)}, u32[]{:S(2)}) copy-start(f32[2,64,1024]{2,1,0:T(8,128)} %copy-done.37) | copy-start | bytes 1572868
  1577.5 73.4 %copy-start.91 = (f32[2,64]{1,0:T(2,128)S(1)}, f32[2,64]{1,0:T(2,128)}, u32[]{:S(2)}) copy-start(f32[2,64]{1,0:T(2,128)} %copy-done.90) | copy-start | bytes 1540
  1577.5 73.4 %copy-start.93 = (f32[2,64]{1,0:T(2,128)S(1)}, f32[2,64]{1,0:T(2,128)}, u32[]{:S(2)}) copy-start(f32[2,64]{1,0:T(2,128)} %copy-done.92) | copy-start | bytes 1540
  (87 other events, 326.8 us)
Sparse Core Ops, SparseCore 0:
  9.6 83.0 all-gather.14
  99.7 74.9 all-gather.24
  177.4 73.1 all-gather.16
  252.0 31.3 all-gather.18
  284.8 103.9 all-gather.20
  390.2 103.9 all-gather.22
  607.7 178.5 reduce-scatter.8
  790.3 177.5 reduce-scatter.6
  970.8 53.3 reduce-scatter.12
  1026.4 189.1 reduce-scatter.14
  1217.9 189.1 reduce-scatter.16
  1409.3 144.4 reduce-scatter.10
  1559.5 443.4 all-reduce.13
where the time goes:
time: 2030 us
  waiting for transfers between devices  1480 us (73%)
  local copies, waits for them, and re-layouts  198 us (10%)
  matrix products  171 us (8%)
  blocking collectives  111 us (5%)
  other arithmetic  51.2 us (3%)
    psum x1, waiting for transfers between devices, body(): lax.psum((lax.psum_scatter(summed[0], 'fsdp', scatter_dimension=0, tiled=...  351 us
    reduce_scatter x2, waiting for transfers between devices, one_batch(): lax.psum_scatter(buffer, 'ctx', scatter_dimension=1, tiled=True)  229 us
    reduce_scatter x1, waiting for transfers between devices, body(): lax.psum_scatter(summed[11], 'fsdp', scatter_dimension=1, tiled=True)  191 us
    reduce_scatter x1, waiting for transfers between devices, body(): lax.psum_scatter(summed[9], 'fsdp', scatter_dimension=0, tiled=True)  191 us
    reduce_scatter x1, waiting for transfers between devices, body(): lax.psum_scatter(summed[2], 'fsdp', scatter_dimension=0, tiled=True)  147 us
    all_gather x1, waiting for transfers between devices, body(): lax.all_gather(shrink_weight, 'fsdp', axis=1, tiled=True)  96.4 us
    all_gather x1, waiting for transfers between devices, body(): lax.all_gather(expand_weight, 'fsdp', axis=0, tiled=True)  85.4 us
    all_gather x2, waiting for transfers between devices, one_batch(): gathered = lax.all_gather(key_value, 'ctx', axis=1, tiled=True)  71.8 us
  transfers between devices with their start and end apart: 13, of which 12 were waited for; matrix products, arithmetic and copies ran while one was open for 14% of the time, Pallas kernels for 0%

commit v1 on v0

--- a/solution.py
+++ b/solution.py
@@ -8,6 +8,17 @@
 MICRO = 2
 EPSILON = 1e-05
 MASKED = -1000000000.0
+
+
+def gather_by_hops(x, axis, dim):
+    peers = lax.axis_size(axis)
+    route = [(i, (i + 1) % peers) for i in range(peers)]
+    parts = [x]
+    for far in range(1, peers):
+        parts = [lax.ppermute(parts[0], axis, route), *parts]
+    whole = jnp.concatenate(parts, axis=dim)
+    shift = (lax.axis_index(axis) + 1) * parts[-1].shape[dim]
+    return jnp.roll(whole, shift, axis=dim)
 
 
 def layer_norm(inputs, norm_gain, norm_bias):
@@ -83,7 +94,7 @@
         ],
         axis=-1,
     ).astype(jnp.bfloat16)
-    gathered = lax.all_gather(key_value, "ctx", axis=1, tiled=True)
+    gathered = gather_by_hops(key_value, "ctx", 1)
     query_heads = queries.reshape(seq_count, row_count, head_count, head_size)
 
     def key_block(number):

time: 2030 us -> 1970 us (0.970)
  waiting for transfers between devices: 1480 us -> 1370 us
    ppermute x0 -> x30, waiting for transfers between devices: none -> 156 us  [gather_by_hops(): parts = [lax.ppermute(parts[0], axis, route), *parts]]
    all_gather x1, waiting for transfers between devices: 96.4 us -> 0.01 us  [body(): lax.all_gather(shrink_weight, 'fsdp', axis=1, tiled=True)]
    all_gather x1, waiting for transfers between devices: 85.4 us -> 0.02 us  [body(): lax.all_gather(expand_weight, 'fsdp', axis=0, tiled=True)]
    all_gather x2 -> x0, waiting for transfers between devices: 71.8 us -> none  [one_batch(): gathered = lax.all_gather(key_value, 'ctx', axis=1, tiled=True)]
    unnamed x258 -> x388, local copies, waits for them, and re-layouts: 56.1 us -> 74.9 us
  transfers between devices with their start and end apart: 13 -> 41, of which waited for: 12 -> 36; matrix products, arithmetic and copies ran while one was open for 14% -> 16% of each run, Pallas kernels for 0% -> 0%
where the time goes in v1:
time: 1970 us; the launch traced here: 1960 us
  waiting for transfers between devices  1370 us (70%)
  local copies, waits for them, and re-layouts  217 us (11%)
  matrix products  171 us (9%)
  blocking collectives  111 us (6%)
  other arithmetic  67.4 us (3%)
    psum x1, waiting for transfers between devices, body(): lax.psum((lax.psum_scatter(summed[0], 'fsdp', scatter_dimension=0, tiled=...  351 us
    reduce_scatter x2, waiting for transfers between devices, one_batch(): lax.psum_scatter(buffer, 'ctx', scatter_dimension=1, tiled=True)  226 us
    reduce_scatter x1, waiting for transfers between devices, body(): lax.psum_scatter(summed[9], 'fsdp', scatter_dimension=0, tiled=True)  192 us
    reduce_scatter x1, waiting for transfers between devices, body(): lax.psum_scatter(summed[11], 'fsdp', scatter_dimension=1, tiled=True)  191 us
    ppermute x30, waiting for transfers between devices, gather_by_hops(): parts = [lax.ppermute(parts[0], axis, route), *parts]  156 us
    reduce_scatter x1, waiting for transfers between devices, body(): lax.psum_scatter(summed[2], 'fsdp', scatter_dimension=0, tiled=True)  147 us
    unnamed x388, local copies, waits for them, and re-layouts  74.9 us
    dynamic_update_slice x8, local copies, waits for them, and re-layouts, key_grads(): lax.dynamic_update_slice_in_dim(running[1], joined_grad, number * size_k, 1)  66.3 us
  transfers between devices with their start and end apart: 41, of which 36 were waited for; matrix products, arithmetic and copies ran while one was open for 16% of the time, Pallas kernels for 0%

profile of v1, /device:TPU:0, one launch (start us, length us, event | category | flops | bytes accessed | tf_op | source)
XLA Modules:
  0.0 1962.9 jit_solution(13701163849002692858)
XLA Ops:
  29.0 63.8 %all-gather.13.cloned.1.call-done = bf16[1024,3072]{1,0:T(8,128)(2,1)} async-done(((bf16[512,3072]{1,0:T(8,128)(2,1)}), bf16[1024,3072]{1,0:T(8,128)(2,1)}) %all-gather.13.cloned.1.call-update) | async-done | bytes 6291472 | tf_op jit(solution)/shard_map/all_gather | solution.py:301
  100.6 9.6 collective-permute-done.15
  144.1 6.4 collective-permute-done.3
  167.4 6.5 collective-permute-done.5
  179.5 5.7 collective-permute-done.6
  190.8 5.7 collective-permute-done.7
  202.1 5.7 collective-permute-done.8
  213.4 5.7 collective-permute-done.9
  230.4 5.7 collective-permute-done.26
  241.8 5.9 collective-permute-done.27
  253.5 5.9 collective-permute-done.28
  306.9 15.7 fusion.54
  322.6 11.9 copy.147
  334.5 16.3 while.122
  350.8 17.3 while.123
  370.2 11.8 copy.137
  382.0 16.2 while.120
  398.3 17.5 while.121
  423.5 6.4 fusion.83
  432.6 8.5 convert_reduce_fusion
  442.1 6.4 fusion.64
  461.8 10.5 while.126
  472.3 8.0 broadcast.731.clone2
  480.2 66.3 %while.127 = (s32[]{:T(128)}, f32[2,64,16,64]{1,3,2,0:T(8,128)}, f32[2,1024,2048]{2,1,0:T(8,128)}, bf16[2,1024,2048]{1,2,0:T(8,128)(2,1)}, s32[1024]{0:T(1024)S(...) while((s32[]{:T(128)}, f32[2,64,16,64]{1,3,2,0:T(8,128)}, ...), condition=%wide.region_37.41_spmd.clone, body=%wide.region_36.40_spmd.clone.sunk | while | flops 685277184 | bytes 136621136 | solution.py:232
  496.9 8.7 copy.231
  505.5 7.8 constant_dynamic-update-slice_fusion.37
  530.1 8.7 copy.231
  538.8 7.7 constant_dynamic-update-slice_fusion.37
  551.7 12.3 while.124
  564.0 9.1 broadcast.731.clone2.1
  573.1 66.9 %while.125 = (s32[]{:T(128)}, f32[2,64,16,64]{1,3,2,0:T(8,128)}, f32[2,1024,2048]{2,1,0:T(8,128)}, bf16[2,1024,2048]{1,2,0:T(8,128)(2,1)}, s32[1024]{0:T(1024)S(...) while((s32[]{:T(128)}, f32[2,64,16,64]{1,3,2,0:T(8,128)}, ...), condition=%wide.region_27.31_spmd.clone, body=%wide.region_26.30_spmd.clone.sunk | while | flops 685277184 | bytes 136621136 | solution.py:232
  589.8 8.9 copy.230
  598.6 7.9 constant_dynamic-update-slice_fusion.36
  623.3 8.9 copy.230
  632.2 7.8 constant_dynamic-update-slice_fusion.36
  648.5 8.3 bitcast_add_fusion.1
  661.9 9.9 bitcast_add_fusion
  675.6 46.0 %reduce-scatter.9.cloned.1.call-done = f32[2,64,2048]{2,1,0:T(8,128)} async-done(((f32[2,1024,2048]{2,1,0:T(8,128)}), f32[2,64,2048]{2,1,0:T(8,128)}) %reduce-scatter.9.cloned.1.call-update) | async-done | bytes 1048592 | tf_op jit(solution)/shard_map/reduce_scatter | solution.py:238
  723.0 180.3 %reduce-scatter.7.cloned.1.call-done = f32[2,64,2048]{2,1,0:T(8,128)} async-done(((f32[2,1024,2048]{2,1,0:T(8,128)}), f32[2,64,2048]{2,1,0:T(8,128)}) %reduce-scatter.7.cloned.1.call-update) | async-done | bytes 1048592 | tf_op jit(solution)/shard_map/reduce_scatter | solution.py:238
  906.6 6.8 bitcast_add_fusion.2
  913.5 46.0 %reduce-scatter.13.cloned.1.call-done = f32[1024,512]{1,0:T(8,128)} async-done(((f32[1024,1024]{1,0:T(8,128)}), f32[1024,512]{1,0:T(8,128)}) %reduce-scatter.13.cloned.1.call-update) | async-done | bytes 2097168 | tf_op jit(solution)/shard_map/reduce_scatter | solution.py:338
  959.5 191.6 %reduce-scatter.15.cloned.1.call-done = f32[512,4096]{1,0:T(8,128)} async-done(((f32[1024,4096]{1,0:T(8,128)}), f32[512,4096]{1,0:T(8,128)}) %reduce-scatter.15.cloned.1.call-update) | async-done | bytes 8388624 | tf_op jit(solution)/shard_map/reduce_scatter | solution.py:342
  1151.1 191.5 %reduce-scatter.17.cloned.1.call-done = f32[4096,512]{1,0:T(8,128)} async-done(((f32[4096,1024]{1,0:T(8,128)}), f32[4096,512]{1,0:T(8,128)}) %reduce-scatter.17.cloned.1.call-update) | async-done | bytes 8388624 | tf_op jit(solution)/shard_map/reduce_scatter | solution.py:344
  1342.5 146.7 %reduce-scatter.11.cloned.1.call-done = f32[512,3072]{1,0:T(8,128)} async-done(((f32[1024,3072]{1,0:T(8,128)}), f32[512,3072]{1,0:T(8,128)}) %reduce-scatter.11.cloned.1.call-update) | async-done | bytes 6291472 | tf_op jit(solution)/shard_map/reduce_scatter | solution.py:335
  1513.3 7.7 all-reduce.11
  1521.6 63.5 %all-reduce.9 = (f32[512]{0:T(512)}, f32[512]{0:T(512)}, f32[512]{0:T(512)}, f32[512]{0:T(512)}, f32[512]{0:T(512)}, /*index=5*/f32[512]{0:T(512)}, f32[512]{0:T(512)}, f32[2048]{0:T(1024)}, f32[512]{0:T(512)}) all-reduce(f32[512]{0:T(512)S(1)} %dynamic-slice.1, ...), channel_id=1, replica_groups=mesh['fsdp'=2,'ctx'=16] {'ctx'}, use_global_device_ids=true, to_apply=%region_44.48 | all-reduce | flops 6144 | bytes 49152 | tf_op jit(solution)/shard_map/psum | solution.py:331
  1587.7 350.7 %all-reduce.14.cloned.1.call-done = (f32[512,3072]{1,0:T(8,128)}, f32[1024,512]{1,0:T(8,128)}, f32[512,4096]{1,0:T(8,128)}, f32[4096,512]{1,0:T(8,128)}) async-done(((f32[512,3072]{1,0:T(8,128)}, f32[1024,512]{1,0:T(8,128)}, f32[512,4096]{1,0:T(8,128)}, f32[4096,512]{1,0:T(8,128)}), (f32[512,3072]{1,0:T(8,128)}, f32[1024,512]{1,0:T(8,128)}, f32[512,4096]{1,0:T(8,128)}, ...) | async-done | bytes 25165840 | tf_op jit(solution)/shard_map/psum | solution.py:331
  1938.4 6.9 copy.328
  (745 shorter events, 417.1 us)
Async XLA Ops:
  7.2 85.5 %all-gather.13.cloned.1.call-start = ((), (), s32[]{:S(2)}) async-start(), calls=%async_computation.6 | async-start | bytes 9437184 | tf_op jit(solution)/shard_map/all_gather | solution.py:301
  8.0 410.2 %all-gather.15.cloned.1.call-start = ((), (), s32[]{:S(2)}) async-start(), calls=%async_computation.7 | async-start | bytes 3145728 | tf_op jit(solution)/shard_map/all_gather | solution.py:304
  8.7 414.8 %all-gather.17.cloned.1.call-start = ((), (), s32[]{:S(2)}) async-start(), calls=%async_computation.8 | async-start | bytes 12582912 | tf_op jit(solution)/shard_map/all_gather | solution.py:308
  9.5 423.1 %all-gather.19.cloned.1.call-start = ((), (), s32[]{:S(2)}) async-start(), calls=%async_computation.9 | async-start | bytes 12582912 | tf_op jit(solution)/shard_map/all_gather | solution.py:310
  98.8 11.4 collective-permute-start.15
  99.0 184.4 %copy-start.155 = (bf16[512]{0:T(512)(128)(2,1)S(1)}, bf16[512]{0:T(512)(128)(2,1)}, u32[]{:S(2)}) copy-start(bf16[512]{0:T(512)(128)(2,1)} %param.50) | copy-start | bytes 3076
  99.0 16.8 collective-permute-start
  110.1 11.3 collective-permute-start.16
  115.8 11.3 collective-permute-start.1
  121.4 11.3 collective-permute-start.17
  127.1 11.3 collective-permute-start.2
  132.7 11.3 collective-permute-start.18
  139.2 11.3 collective-permute-start.3
  144.1 12.0 collective-permute-start.19
  150.5 11.3 collective-permute-start.4
  156.1 11.3 collective-permute-start.20
  162.6 11.3 collective-permute-start.5
  167.4 12.1 collective-permute-start.21
  173.9 11.3 collective-permute-start.6
  179.5 11.3 collective-permute-start.22
  185.2 11.3 collective-permute-start.7
  190.8 11.3 collective-permute-start.23
  196.5 11.3 collective-permute-start.8
  202.1 11.3 collective-permute-start.24
  207.8 11.3 collective-permute-start.9
  213.4 11.3 collective-permute-start.25
  219.1 11.3 collective-permute-start.10
  224.7 11.4 collective-permute-start.26
  230.4 11.4 collective-permute-start.11
  236.2 11.6 collective-permute-start.27
  236.2 485.5 %reduce-scatter.9.cloned.1.call-start = ((), (), s32[]{:S(2)}) async-start(), calls=%async_computation.11 | async-start | bytes 17825792 | tf_op jit(solution)/shard_map/reduce_scatter | solution.py:238
  241.8 11.6 collective-permute-start.12
  247.8 11.6 collective-permute-start.28
  253.5 36.9 %collective-permute-start.13 = (bf16[2,64,2048]{2,1,0:T(8,128)(2,1)}, bf16[2,64,2048]{2,1,0:T(8,128)(2,1)}, u32[]{:S(2)}, u32[]{:S(2)}) collective-permute-start(bf16[2,64,2048]{2,1,0:T(8,128)(2,1)} %collective-permute-done.12), channel_id=1, source_target_pairs={{0,1},{1,2},{2,3},{3,4},{4,5},{5,6},{6,7},{7,8},{8,9},{9,10},{10,1... | collective-permute-start | bytes 1572872 | tf_op jit(solution)/shard_map/ppermute | solution.py:18
  259.4 31.0 %collective-permute-start.29 = (bf16[2,64,2048]{2,1,0:T(8,128)(2,1)}, bf16[2,64,2048]{2,1,0:T(8,128)(2,1)}, u32[]{:S(2)}, u32[]{:S(2)}) collective-permute-start(bf16[2,64,2048]{2,1,0:T(8,128)(2,1)} %collective-permute-done.28), channel_id=1, source_target_pairs={{0,1},{1,2},{2,3},{3,4},{4,5},{5,6},{6,7},{7,8},{8,9},{9,10},{10,1... | collective-permute-start | bytes 1572872 | tf_op jit(solution)/shard_map/ppermute | solution.py:18
  290.3 11.6 collective-permute-start.14
  546.6 356.7 %reduce-scatter.7.cloned.1.call-start = ((), (), s32[]{:S(2)}) async-start(), calls=%async_computation.10 | async-start | bytes 17825792 | tf_op jit(solution)/shard_map/reduce_scatter | solution.py:238
  640.0 319.5 %reduce-scatter.13.cloned.1.call-start = ((), (), s32[]{:S(2)}) async-start(), calls=%async_computation.13 | async-start | bytes 6291456 | tf_op jit(solution)/shard_map/reduce_scatter | solution.py:338
  644.7 506.4 %reduce-scatter.15.cloned.1.call-start = ((), (), s32[]{:S(2)}) async-start(), calls=%async_computation.14 | async-start | bytes 25165824 | tf_op jit(solution)/shard_map/reduce_scatter | solution.py:342
  656.9 685.7 %reduce-scatter.17.cloned.1.call-start = ((), (), s32[]{:S(2)}) async-start(), calls=%async_computation.15 | async-start | bytes 25165824 | tf_op jit(solution)/shard_map/reduce_scatter | solution.py:344
  671.8 232.8 %copy-start.15 = (bf16[4,64,1024]{2,1,0:T(8,128)(2,1)S(1)}, bf16[4,64,1024]{2,1,0:T(8,128)(2,1)}, u32[]{:S(2)}) copy-start(bf16[4,64,1024]{2,1,0:T(8,128)(2,1)} %param.39) | copy-start | bytes 1572868
  671.9 232.7 %copy-start.52 = (f32[2,1,512]{2,1,0:T(1,128)S(1)}, f32[2,1,512]{2,1,0:T(1,128)}, u32[]{:S(2)}) copy-start(f32[2,1,512]{2,1,0:T(1,128)} %copy-done.51) | copy-start | bytes 12292
  671.9 232.7 %copy-start.58 = (f32[2,1,512]{2,1,0:T(1,128)S(1)}, f32[2,1,512]{2,1,0:T(1,128)}, u32[]{:S(2)}) copy-start(f32[2,1,512]{2,1,0:T(1,128)} %copy-done.57) | copy-start | bytes 12292
  671.9 232.7 %copy-start.116 = (f32[2,64]{1,0:T(2,128)S(1)}, f32[2,64]{1,0:T(2,128)}, u32[]{:S(2)}) copy-start(f32[2,64]{1,0:T(2,128)} %copy-done.115) | copy-start | bytes 1540
  671.9 232.7 %copy-start.126 = (f32[2,64]{1,0:T(2,128)S(1)}, f32[2,64]{1,0:T(2,128)}, u32[]{:S(2)}) copy-start(f32[2,64]{1,0:T(2,128)} %copy-done.125) | copy-start | bytes 1540
  671.9 817.4 %reduce-scatter.11.cloned.1.call-start = ((), (), s32[]{:S(2)}) async-start(), calls=%async_computation.12 | async-start | bytes 18874368 | tf_op jit(solution)/shard_map/reduce_scatter | solution.py:335
  675.6 231.0 %copy-start.61 = (bf16[2,64,1024]{2,1,0:T(8,128)(2,1)}, bf16[2,64,1024]{2,1,0:T(8,128)(2,1)S(1)}, u32[]{:S(2)}) copy-start(bf16[2,64,1024]{2,1,0:T(8,128)(2,1)S(1)} %copy.186) | copy-start | bytes 786436
  913.5 1025.0 %all-reduce.14.cloned.1.call-start = ((), (), s32[]{:S(2)}) async-start(), calls=%async_computation.16 | async-start | bytes 50331648 | tf_op jit(solution)/shard_map/psum | solution.py:331
  (165 other events, 3559.9 us)
Sparse Core Ops, SparseCore 0:
  9.6 83.0 all-gather.12
  94.3 33.1 all-gather.14
  129.0 103.9 all-gather.16
  236.3 104.4 all-gather.18
  546.6 174.9 reduce-scatter.8
  725.6 177.6 reduce-scatter.6
  906.2 53.3 reduce-scatter.12
  961.9 189.1 reduce-scatter.14
  1153.4 189.1 reduce-scatter.16
  1344.8 144.4 reduce-scatter.10
  1494.9 443.4 all-reduce.13
